TPU v7x, 256 devices: a whole 4x4x8 slice. The times are simulated.
256 devices in a mesh: layer: 2 (over core), row: 8 (over z_hi, y), col: 16 (over x, z_lo).
Axes of the slice: x: 4, y: 4, z: 8 (z_hi: 2, z_lo: 4; z = z_hi * 4 + z_lo), core: 2. Of those that a mesh axis runs over, the one named last changes fastest.
Arguments:
- amplitudes: bfloat16 [512, 128, 128], P(('row', 'col')), may hold values from -6 to 6
- integrals: bfloat16 [32768, 128, 128], P(('layer', 'row', 'col')), may hold values from -0.1875 to 0.1875
- amp_index: int32 [4096, 48], P(('layer', 'row', 'col')), may hold values from 0 to 31
- left_index: int32 [4096, 48], P(('layer', 'row', 'col')), may hold values from 0 to 127, as said below
- right_index: int32 [4096, 48], P(('layer', 'row', 'col')), may hold values from 0 to 127, as said below
- dest_col: int32 [2048, 1], P(('row', 'col')), may hold values from 0 to 15; in each aligned block of 16 rows (0 to 15, 16 to 31, ...) at most 2 rows name the same one
- owner_slot: int32 [2048], P(('row', 'col')), may hold values from 0 to 7
Outputs:
- ladder: float32 [1024, 128, 128], P(('row', 'col'))
Inputs may be any that keep to these rules, and one draw needn't show every extreme that they name: `dest_col`: among the 16 result tiles of one index of row and col, no owner column appears more than 2 times, and some column appears exactly 2 times. A term's amplitude tile is number amp_index among the tiles of the devices with the same col index, counted row by row. A term's left and right integral tiles belong to one auxiliary function: left_index // 2 == right_index // 2. right_index // 2 == left_index // 2 for every term.
All inputs are finite; a program needn't handle non-finite values.
Results may differ from a plain program's by a relative error of at most 0.0029.
Values may be sent and summed in bfloat16 or wider, within the bound.
A program may use at most 64 MiB of HBM per device.

v0:
```python
import jax
import jax.numpy as jnp
from jax import lax
from jax.sharding import PartitionSpec as P

OWN = 8
CAP = 2


def select_tiles(stack_flat, picks, count, tile_edge):
    onehot = (picks[:, None] == jnp.arange(count, dtype=jnp.int32)[None, :]).astype(jnp.bfloat16)
    chosen = jnp.dot(onehot, stack_flat, preferred_element_type=jnp.float32).astype(jnp.bfloat16)
    return chosen.reshape(picks.shape[0], tile_edge, tile_edge)


def shards(amplitudes, integrals, amp_index, left_index, right_index, dest_col, owner_slot):
    columns = lax.axis_size("col")
    slot_count = dest_col.shape[0]
    tile_edge = integrals.shape[1]
    gathered = lax.all_gather(amplitudes, "row", axis=0, tiled=True)
    amp_total = gathered.shape[0]
    int_total = integrals.shape[0]
    amp_flat = gathered.reshape(amp_total, tile_edge * tile_edge)
    int_flat = integrals.reshape(int_total, tile_edge * tile_edge)

    def one_slot(operand_list):
        amp_ids, left_ids, right_ids = operand_list
        amp_tiles = select_tiles(amp_flat, amp_ids, amp_total, tile_edge)
        right_tiles = select_tiles(int_flat, right_ids, int_total, tile_edge)
        middle_product = jnp.einsum(
            "tcd,ted->tce", amp_tiles, right_tiles, preferred_element_type=jnp.float32
        ).astype(jnp.bfloat16)
        left_tile_blocks = select_tiles(int_flat, left_ids, int_total, tile_edge)
        return jnp.einsum(
            "dov,dvh->oh", left_tile_blocks, middle_product, preferred_element_type=jnp.float32
        )

    partials = lax.map(one_slot, (amp_index, left_index, right_index))
    target = dest_col[:, 0]
    counter = jnp.arange(slot_count, dtype=jnp.int32)
    earlier = (target[:, None] == target[None, :]) & (counter[None, :] < counter[:, None])
    position_in = jnp.sum(earlier.astype(jnp.int32), axis=1)
    position = target * CAP + position_in
    placing = (position[None, :] == jnp.arange(columns * CAP, dtype=jnp.int32)[:, None]).astype(
        jnp.float32
    )
    buffer = jnp.dot(
        placing,
        partials.reshape(slot_count, tile_edge * tile_edge),
        precision=lax.Precision.HIGHEST,
        preferred_element_type=jnp.float32,
    )
    buffer = buffer.reshape(columns, CAP, tile_edge, tile_edge)
    labels = (
        jnp.full((columns * CAP,), OWN, jnp.int32)
        .at[position]
        .set(owner_slot)
        .reshape(columns, CAP)
    )
    tiles_in, labels_in = (
        lax.all_to_all(buffer, "col", split_axis=0, concat_axis=0, tiled=True),
        lax.all_to_all(labels, "col", split_axis=0, concat_axis=0, tiled=True),
    )
    flattened = tiles_in.reshape(-1, tile_edge * tile_edge)
    owner_mask = (
        labels_in.reshape(-1)[:, None] == jnp.arange(OWN, dtype=jnp.int32)[None, :]
    ).astype(jnp.float32)
    owned_tiles = jnp.dot(
        owner_mask.T, flattened, precision=lax.Precision.HIGHEST, preferred_element_type=jnp.float32
    )
    owned_tiles = lax.psum(owned_tiles, "layer")
    return owned_tiles.reshape(OWN, tile_edge, tile_edge)


def solution(mesh):
    placed = (
        P(("row", "col"), None, None),
        P(("layer", "row", "col"), None, None),
        P(("layer", "row", "col"), None),
        P(("layer", "row", "col"), None),
        P(("layer", "row", "col"), None),
        P(("row", "col"), None),
        P(("row", "col")),
    )
    return jax.shard_map(
        shards, mesh=mesh, in_specs=placed, out_specs=P(("row", "col"), None, None), check_vma=False
    )
```

profile of v0, /device:TPU:1, one launch (start us, length us, event | category | flops | bytes accessed | tf_op | source)
XLA Modules:
  0.0 384.1 jit_solution(10383428219554340299)
XLA Ops:
  10.3 9.0 %all-to-all-start = ((s32[16,1,2]{2,1,0:T(1,128)}), s32[16,1,2]{2,1,0:T(1,128)S(1)}, u32[]{:S(2)}, u32[]{:S(2)}) async-start(s32[16,1,2]{2,1,0:T(1,128)} %bitcast.8), calls=%async_computation | async-start | bytes 16384 | tf_op jit(solution)/shard_map/all_to_all | solution.py:62
  19.3 7.7 %copy.44 = bf16[16,8,128,128]{3,1,2,0:T(8,128)(2,1)} copy(bf16[16,8,128,128]{3,2,1,0:T(8,128)(2,1)} %bitcast.108) | data formatting | bytes 8388608
  27.0 47.3 %all-gather.2.cloned.1.call-done = bf16[32,128,128]{2,1,0:T(8,128)(2,1)} async-done(((bf16[4,128,128]{2,1,0:T(8,128)(2,1)}), bf16[32,128,128]{2,1,0:T(8,128)(2,1)}) %all-gather.2.cloned.1.call-update) | async-done | bytes 1048592 | tf_op jit(solution)/shard_map/all_gather | solution.py:20
  74.3 2.9 copy.45
  77.2 210.3 %while.10 = (s32[]{:T(128)}, f32[16,128,128]{2,1,0:T(8,128)}, s32[16,48]{1,0:T(8,128)}, bf16[128,16384]{1,0:T(8,128)(2,1)}, s32[16,48]{1,0:T(8,128)}, /*index=5*...) while((s32[]{:T(128)}, f32[16,128,128]{2,1,0:T(8,128)}, s32[16,48]{1,0:T(8,128)}, ...), condition=%wide.region_3.4_spmd, body=%wide.region_2.3_spmd.sunk | while | flops 858797568 | bytes 45156664 | solution.py:38
  77.9 2.9 fusion.54
  86.7 3.7 fusion.58
  91.1 2.9 fusion.54
  99.8 3.7 fusion.58
  104.2 2.9 fusion.54
  107.6 2.0 fusion.55
  113.0 3.7 fusion.58
  117.3 2.9 fusion.54
  126.1 3.7 fusion.58
  130.5 2.9 fusion.54
  139.3 3.7 fusion.58
  143.6 2.9 fusion.54
  152.4 3.7 fusion.58
  156.8 2.9 fusion.54
  160.1 2.0 fusion.55
  165.6 3.7 fusion.58
  169.9 2.9 fusion.54
  178.7 3.7 fusion.58
  183.1 2.9 fusion.54
  191.9 3.7 fusion.58
  196.2 2.9 fusion.54
  199.6 2.0 fusion.55
  205.0 3.7 fusion.58
  209.4 2.9 fusion.54
  218.1 3.7 fusion.58
  222.5 2.9 fusion.54
  225.9 2.0 fusion.55
  231.3 3.7 fusion.58
  235.7 2.9 fusion.54
  239.0 2.0 fusion.55
  244.4 3.7 fusion.58
  248.8 2.9 fusion.54
  257.6 3.7 fusion.58
  262.0 2.9 fusion.54
  265.3 2.0 fusion.55
  270.7 3.7 fusion.58
  275.1 2.9 fusion.54
  283.9 3.7 fusion.58
  287.5 2.7 fusion.18
  292.2 4.5 %all-to-all-start.1 = ((f32[16,2,128,128]{3,2,1,0:T(8,128)}), f32[16,2,128,128]{3,2,1,0:T(8,128)S(1)}, u32[]{:S(2)}, u32[]{:S(2)}) async-start(f32[16,2,128,128]{3,2,1,0:T(8,128)} %copy.18), calls=%async_computation.1 | async-start | bytes 4194304 | tf_op jit(solution)/shard_map/all_to_all | solution.py:61
  298.2 48.2 %all-to-all-done.1 = f32[16,2,128,128]{3,2,1,0:T(8,128)S(1)} async-done(((f32[16,2,128,128]{3,2,1,0:T(8,128)}), f32[16,2,128,128]{3,2,1,0:T(8,128)S(1)}, u32[]{:S(2)}, u32[]{:S(2)}) %all-to-all-start.1) | async-done | bytes 2097184 | tf_op jit(solution)/shard_map/all_to_all | solution.py:61
  346.5 2.0 fusion.15
  349.4 26.0 %all-reduce.2.cloned.1.call-done = f32[8,128,128]{2,1,0:T(8,128)} async-done(((f32[8,128,128]{2,1,0:T(8,128)}), f32[8,128,128]{2,1,0:T(8,128)}) %all-reduce.2.cloned.1.call-update) | async-done | bytes 524304 | tf_op jit(solution)/shard_map/psum | solution.py:71
  (158 shorter events, 102.3 us)
Async XLA Ops:
  6.5 67.8 %all-gather.2.cloned.1.call-start = ((), (), s32[]{:S(2)}) async-start(), calls=%async_computation.2 | async-start | bytes 1179648 | tf_op jit(solution)/shard_map/all_gather | solution.py:20
  10.3 281.9 %all-to-all-start = ((s32[16,1,2]{2,1,0:T(1,128)}), s32[16,1,2]{2,1,0:T(1,128)S(1)}, u32[]{:S(2)}, u32[]{:S(2)}) async-start(s32[16,1,2]{2,1,0:T(1,128)} %bitcast.8), calls=%async_computation | async-start | bytes 16384 | tf_op jit(solution)/shard_map/all_to_all | solution.py:62
  19.3 7.7 %copy-start.1 = (s32[16,1]{0,1:T(1,128)S(1)}, s32[16,1]{0,1:T(1,128)}, u32[]{:S(2)}) copy-start(s32[16,1]{0,1:T(1,128)} %param.14) | copy-start | bytes 196
  81.2 3.1 copy-start
  94.4 3.1 copy-start
  107.5 3.1 copy-start
  120.7 3.1 copy-start
  133.8 3.1 copy-start
  147.0 3.1 copy-start
  160.1 3.1 copy-start
  173.3 3.1 copy-start
  186.4 3.1 copy-start
  199.6 3.1 copy-start
  212.7 3.1 copy-start
  225.8 3.1 copy-start
  239.0 3.1 copy-start
  252.1 3.1 copy-start
  265.3 3.1 copy-start
  278.4 3.1 copy-start
  292.2 54.3 %all-to-all-start.1 = ((f32[16,2,128,128]{3,2,1,0:T(8,128)}), f32[16,2,128,128]{3,2,1,0:T(8,128)S(1)}, u32[]{:S(2)}, u32[]{:S(2)}) async-start(f32[16,2,128,128]{3,2,1,0:T(8,128)} %copy.18), calls=%async_computation.1 | async-start | bytes 4194304 | tf_op jit(solution)/shard_map/all_to_all | solution.py:61
  296.7 78.7 %all-reduce.2.cloned.1.call-start = ((), (), s32[]{:S(2)}) async-start(), calls=%async_computation.3 | async-start | bytes 1048576 | tf_op jit(solution)/shard_map/psum | solution.py:71
Sparse Core Ops, SparseCore 0:
  10.0 64.2 all-gather.1
  349.6 25.8 all-reduce.1
where the time goes:
time: 386 us; the launch traced here: 384 us
  matrix products  153 us (40%)
  waiting for transfers between devices  122 us (32%)
  local copies, waits for them, and re-layouts  78.2 us (20%)
  starting transfers between devices  13.8 us (4%)
  between operations  13.5 us (3%)
    dot_general x48, matrix products, select_tiles(): jnp.dot(onehot, stack_flat, preferred_element_type=jnp.float32)  90.2 us
    dot_general x16, matrix products, one_slot(): jnp.einsum('dov,dvh->oh', left_tile_blocks, middle_product, preferred_ele...  58.6 us
    all_to_all x1, waiting for transfers between devices, shards(): lax.all_to_all(buffer, 'col', split_axis=0, concat_axis=0, tiled=True)  48.2 us
    all_gather x1, waiting for transfers between devices, shards(): gathered = lax.all_gather(amplitudes, 'row', axis=0, tiled=True)  47.3 us
    while x80, local copies, waits for them, and re-layouts  38.3 us
    psum x1, waiting for transfers between devices, shards(): owned_tiles = lax.psum(owned_tiles, 'layer')  26 us
    eq x32, local copies, waits for them, and re-layouts, select_tiles(): picks[:, None] == jnp.arange(count, dtype=jnp.int32)[None, :]  22.5 us
    unnamed x5, local copies, waits for them, and re-layouts  12.5 us
  transfers between devices with their start and end apart: 4, of which 3 were waited for; matrix products, arithmetic and copies ran while one was open for 59% of the time, Pallas kernels for 0%

commit v1 on v0

v1 whole, which is shorter than its diff:
```python
import jax
import jax.numpy as jnp
from jax import lax
from jax.experimental import pallas as pl
from jax.experimental.pallas import tpu as pltpu
from jax.sharding import PartitionSpec as P

MESH = pl.DeviceIdType.MESH
OWN = 8
AMP = 4
X, Y, ZLO = 4, 4, 4
COLS = X * ZLO
EARLY = COLS // 2
CHUNKS = 4


def product(left, right):
    return jnp.dot(left, right, preferred_element_type=jnp.float32)


def flip(bit):
    return 1 - bit


def other_half(row, far):
    return lax.rem(row + far * Y, 2 * Y)


def next_y(row, step):
    return (row // Y) * Y + lax.rem(row + step, Y)


def destination(col, place):
    x, z = col // ZLO, col % ZLO
    half, swap, dx = flip(place // EARLY), (place % EARLY) // X, place % X
    z = lax.rem(z + 2 * half, ZLO)
    z = z + swap * (1 - 2 * (z % 2))
    return lax.rem(x + dx, X) * ZLO + z


def kernel(amp_ix, left_ix, right_ix, dest, slot, amp_hbm, int_hbm, out,
           amps, ints, turned, part, stage_s, stage_i, got_s, got_i, got_f, tags, tags_in,
           order, first, count,
           local_sem, y_send, y_recv, z_send, z_recv, zy_send, zy_recv, f_send, f_recv,
           s_send, s_recv, i_send, i_recv, b_send, b_recv, t_send, t_recv):
    layer, row, col = lax.axis_index("layer"), lax.axis_index("row"), lax.axis_index("col")
    slots, terms = amp_ix.shape
    tiles = int_hbm.shape[0]
    edge = int_hbm.shape[1]
    half = AMP // 2
    mine = half * layer
    mate = {"layer": flip(layer)}
    far = other_half(row, 1)

    barrier = pltpu.get_barrier_semaphore()
    peers = [mate, {"row": far}]
    peers += [{"row": next_y(row, s)} for s in range(1, Y)]
    for peer in peers:
        pl.semaphore_signal(barrier, inc=1, device_id=peer, device_id_type=MESH)
    for place in range(COLS):
        if place != EARLY:
            pl.semaphore_signal(barrier, inc=1, device_id={"col": destination(col, place)}, device_id_type=MESH)

    own_amp = pltpu.make_async_copy(amp_hbm, amps.at[pl.ds(row * AMP, AMP)], local_sem.at[CHUNKS])
    own_amp.start()
    loads = []
    step = tiles // CHUNKS
    for c in range(CHUNKS):
        loads.append(pltpu.make_async_copy(int_hbm.at[pl.ds(c * step, step)], ints.at[pl.ds(c * step, step)], local_sem.at[c]))
        loads[-1].start()

    x, z = col // ZLO, col % ZLO

    def place_of(k):
        to = dest[k, 0]
        dx = lax.rem(to // ZLO - x + X, X)
        zt = lax.rem(to, ZLO)
        same = jnp.where(zt // 2 == z // 2, 1, 0)
        swap = jnp.where(zt % 2 == z % 2, 0, 1)
        return same * EARLY + swap * X + dx

    places = [place_of(k) for k in range(slots)]
    ranks = []
    for k in range(slots):
        rank = 0
        for j in range(slots):
            if j < k:
                rank = rank + jnp.where(places[j] <= places[k], 1, 0)
            elif j > k:
                rank = rank + jnp.where(places[j] < places[k], 1, 0)
        ranks.append(rank)
    for i in range(slots):
        at, below, same = 0, 0, 0
        for k in range(slots):
            at = at + jnp.where(ranks[k] == i, k, 0)
            below = below + jnp.where(places[k] < i, 1, 0)
            same = same + jnp.where(places[k] == i, 1, 0)
        order[i] = at
        first[i] = below
        count[i] = same

    def pick(place, j):
        at = jnp.minimum(first[place] + j, slots - 1)
        return at, j < count[place]

    def tag(place, _):
        for j in range(2):
            at, there = pick(place, j)
            tags[place, j] = jnp.full((8, edge), jnp.where(there, slot[order[at]], OWN), jnp.int32)
        return 0

    lax.fori_loop(0, COLS, tag, 0)

    def turn(c):
        loads[c].wait()

        def four(i, _):
            for j in range(4):
                turned[c * step + 4 * i + j] = ints[c * step + 4 * i + j].T
            return 0

        lax.fori_loop(0, step // 4, four, 0)

    turn(0)
    own_amp.wait()
    pl.semaphore_wait(barrier, len(peers) + COLS - 1)

    def block(r, n=half, at=0):
        return amps.at[pl.ds(r * AMP + mine + at, n)]

    def send(src, dst, out_sem, in_sem, peer):
        return pltpu.make_async_remote_copy(
            src_ref=src, dst_ref=dst, send_sem=out_sem, recv_sem=in_sem, device_id=peer, device_id_type=MESH
        )

    z_copies = [send(block(row, 1, t), block(row, 1, t), z_send.at[t], z_recv.at[t], {"row": far}) for t in range(half)]
    for c in z_copies:
        c.start()
    y_copies = [
        send(block(row), block(row), y_send.at[s - 1], y_recv.at[s - 1], {"row": next_y(row, s)}) for s in (1, 3, 2)
    ]
    for c in y_copies:
        c.start()
    tag_copies = []
    for place in range(COLS):
        if place != EARLY:
            tag_copies.append(send(tags.at[place], tags_in.at[place], t_send.at[place], t_recv.at[place],
                                   {"col": destination(col, place)}))
            tag_copies[-1].start()
    for c in range(1, CHUNKS):
        turn(c)

    to_mate = []

    def forward(r, n, at, k):
        to_mate.append(send(block(r, n, at), block(r, n, at), f_send.at[k], f_recv.at[k], mate))
        to_mate[-1].start()

    def arrived(r, n, at, sem):
        send(block(r, n, at), block(r, n, at), f_send.at[0], sem, mate).wait_recv()

    came = []
    k = 0
    for s in (1, 3, 2):
        r = next_y(row, Y - s)
        arrived(r, half, 0, y_recv.at[s - 1])
        forward(r, half, 0, k)
        came.append((r, half, 0, k))
        k += 1
    zy_copies = []
    for t in range(half):
        arrived(far, 1, t, z_recv.at[t])
        for s in (2, 1, 3):
            zy_copies.append(send(block(far, 1, t), block(far, 1, t), zy_send.at[t, s - 1], zy_recv.at[t, s - 1],
                                  {"row": next_y(row, s)}))
            zy_copies[-1].start()
        forward(far, 1, t, k)
        came.append((far, 1, t, k))
        k += 1
    for t in range(half):
        for s in (1, 3, 2):
            r = next_y(far, Y - s)
            arrived(r, 1, t, zy_recv.at[t, s - 1])
            forward(r, 1, t, k)
            came.append((r, 1, t, k))
            k += 1

    def of_mate(r, n, at):
        return amps.at[pl.ds(r * AMP + half * flip(layer) + at, n)]

    for r, n, at, k in came:
        send(of_mate(r, n, at), of_mate(r, n, at), f_send.at[0], f_recv.at[k], mate).wait_recv()
    for c in z_copies + y_copies + zy_copies + to_mate:
        c.wait_send()

    def s_copy(p):
        return send(stage_s.at[p], got_s.at[p], s_send.at[p], s_recv.at[p], mate)

    def i_copy(p):
        return send(stage_i.at[p], got_i.at[p], i_send.at[p], i_recv.at[p], {"col": destination(col, p)})

    def b_copy(p):
        return send(got_i.at[p], got_f.at[p], b_send.at[p], b_recv.at[p], mate)

    def chosen(p, j):
        at, there = pick(p, j)
        return part[at] * jnp.where(there, 1.0, 0.0)

    def to_sibling(p):
        stage_s[p] = chosen(p, flip(layer)).astype(jnp.bfloat16)
        s_copy(p).start()

    def both(p):
        s_copy(p).wait_recv()
        return (chosen(p, layer) + got_s[p].astype(jnp.float32)).astype(jnp.bfloat16)

    def to_owner(p):
        stage_i[p] = both(p)
        i_copy(p).start()

    def result(i):
        k = order[i]
        middles, lefts = [], []
        for t in range(terms):
            middles.append(product(amps[amp_ix[k, t]], turned[right_ix[k, t]]).astype(jnp.bfloat16))
            lefts.append(ints[left_ix[k, t]])
        part[i] = product(jnp.concatenate(lefts, 1), jnp.concatenate(middles, 0))

    def two(i, _):
        @pl.when(i >= 1)
        def _():
            to_sibling(i - 1)

        @pl.when(i >= 2)
        def _():
            to_owner(i - 2)

        result(2 * i)
        result(2 * i + 1)
        return 0

    lax.fori_loop(0, slots // 2, two, 0)

    def rest(p, _):
        to_sibling(p)
        return 0

    lax.fori_loop(EARLY - 1, COLS, rest, 0)
    to_owner(EARLY - 2)
    to_owner(EARLY - 1)
    got_i[EARLY] = both(EARLY)

    def rest_owner(p, _):
        to_owner(p)
        return 0

    lax.fori_loop(EARLY + 1, COLS, rest_owner, 0)
    b_copy(EARLY).start()

    def onward(p, _):
        i_copy(p).wait_recv()
        b_copy(p).start()
        return 0

    lax.fori_loop(0, EARLY, onward, 0)
    for place in range(COLS):
        if place != EARLY:
            send(tags.at[place], tags_in.at[place], t_send.at[place], t_recv.at[place], mate).wait_recv()
    tags_in[EARLY] = tags[EARLY]
    out[...] = jnp.zeros_like(out)

    def add(p, ref, j):
        label = tags_in[p, j]
        tile = ref[p].astype(jnp.float32).reshape(edge // 8, 8, edge)
        for s in range(OWN):
            there = jnp.where(label == s, 1.0, 0.0)
            out[s] += (tile * there[None]).reshape(edge, edge)

    def add_own(p, _):
        add(p, got_i, layer)
        return 0

    def add_mate(p, _):
        b_copy(p).wait_recv()
        add(p, got_f, flip(layer))
        return 0

    lax.fori_loop(0, EARLY + 1, add_own, 0)
    lax.fori_loop(0, EARLY + 1, add_mate, 0)

    lax.fori_loop(EARLY + 1, COLS, onward, 0)
    lax.fori_loop(EARLY + 1, COLS, add_own, 0)
    lax.fori_loop(EARLY + 1, COLS, add_mate, 0)

    def drain(p, _):
        s_copy(p).wait_send()
        b_copy(p).wait_send()
        return 0

    lax.fori_loop(0, COLS, drain, 0)
    for place in range(COLS):
        if place != EARLY:
            i_copy(place).wait_send()
    for c in tag_copies:
        c.wait_send()


def shards(amplitudes, integrals, amp_index, left_index, right_index, dest_col, owner_slot):
    edge = integrals.shape[1]
    half = AMP // 2
    rows = lax.axis_size("row")
    tile = (edge, edge)
    dma = pltpu.SemaphoreType.DMA
    in_smem = pl.BlockSpec(memory_space=pltpu.SMEM)
    in_hbm = pl.BlockSpec(memory_space=pl.ANY)
    forwards = 3 + half + 3 * half
    return pl.pallas_call(
        kernel,
        out_shape=jax.ShapeDtypeStruct((OWN, *tile), jnp.float32),
        in_specs=[in_smem] * 5 + [in_hbm] * 2,
        out_specs=pl.BlockSpec(memory_space=pltpu.VMEM),
        scratch_shapes=[
            pltpu.VMEM((rows * AMP, *tile), jnp.bfloat16),
            pltpu.VMEM(integrals.shape, jnp.bfloat16),
            pltpu.VMEM(integrals.shape, jnp.bfloat16),
            pltpu.VMEM((COLS, *tile), jnp.float32),
            pltpu.VMEM((COLS, *tile), jnp.bfloat16),
            pltpu.VMEM((COLS, *tile), jnp.bfloat16),
            pltpu.VMEM((COLS, *tile), jnp.bfloat16),
            pltpu.VMEM((COLS, *tile), jnp.bfloat16),
            pltpu.VMEM((COLS, *tile), jnp.bfloat16),
            pltpu.VMEM((COLS, 2, 8, edge), jnp.int32),
            pltpu.VMEM((COLS, 2, 8, edge), jnp.int32),
            pltpu.SMEM((COLS,), jnp.int32),
            pltpu.SMEM((COLS,), jnp.int32),
            pltpu.SMEM((COLS,), jnp.int32),
            dma((CHUNKS + 1,)),
            dma((3,)), dma((3,)),
            dma((half,)), dma((half,)),
            dma((half, 3)), dma((half, 3)),
            dma((forwards,)), dma((forwards,)),
            dma((COLS,)), dma((COLS,)),
            dma((COLS,)), dma((COLS,)),
            dma((COLS,)), dma((COLS,)),
            dma((COLS,)), dma((COLS,)),
        ],
        compiler_params=pltpu.CompilerParams(collective_id=0, has_side_effects=True),
    )(amp_index, left_index, right_index, dest_col, owner_slot, amplitudes, integrals)


def solution(mesh):
    placed = (
        P(("row", "col"), None, None),
        P(("layer", "row", "col"), None, None),
        P(("layer", "row", "col"), None),
        P(("layer", "row", "col"), None),
        P(("layer", "row", "col"), None),
        P(("row", "col"), None),
        P(("row", "col")),
    )
    return jax.shard_map(
        shards, mesh=mesh, in_specs=placed, out_specs=P(("row", "col"), None, None), check_vma=False
    )
```

time: 386 us -> 54.3 us (0.14)
  matrix products: 153 us -> 0 us
  waiting for transfers between devices: 122 us -> 0 us
  local copies, waits for them, and re-layouts: 78.2 us -> 3.2 us
  Pallas kernels: 0 us -> 50.9 us
  starting transfers between devices: 13.8 us -> 0 us
  between operations: 13.5 us -> 0.01 us
    dot_general x66 -> x0, matrix products: 153 us -> none  [the longest x48 90.2 us: select_tiles(): jnp.dot(onehot, stack_flat, preferred_element_type=jnp.float32)]
    pallas_call x0 -> x1, Pallas kernels: none -> 50.9 us  [shards(): pl.pallas_call(kernel, out_shape=jax.ShapeDtypeStruct((OWN, *tile), jnp.f...]
    all_to_all x2 -> x0, waiting for transfers between devices: 48.2 us -> none  [the longest x1 48.2 us: shards(): lax.all_to_all(buffer, 'col', split_axis=0, concat_axis=0, tiled=True)]
    all_gather x1 -> x0, waiting for transfers between devices: 47.3 us -> none  [shards(): gathered = lax.all_gather(amplitudes, 'row', axis=0, tiled=True)]
    while x80 -> x0, local copies, waits for them, and re-layouts: 38.3 us -> none
    psum x1 -> x0, waiting for transfers between devices: 26 us -> none  [shards(): owned_tiles = lax.psum(owned_tiles, 'layer')]
    eq x33 -> x0, local copies, waits for them, and re-layouts: 22.6 us -> none  [the longest x32 22.5 us: select_tiles(): picks[:, None] == jnp.arange(count, dtype=jnp.int32)[None, :]]
    all_to_all x2 -> x0, starting transfers between devices: 13.5 us -> none  [the longest x1 9.01 us: shards(): lax.all_to_all(labels, 'col', split_axis=0, concat_axis=0, tiled=True)]
  transfers between devices with their start and end apart: 4 -> 0, of which waited for: 3 -> 0; matrix products, arithmetic and copies ran while one was open for 59% -> 0% of each run, Pallas kernels for 0% -> 0%
where the time goes in v1:
time: 54.3 us; the launch traced here: 54.1 us
  Pallas kernels  50.9 us (94%)
  local copies, waits for them, and re-layouts  3.2 us (6%)
    pallas_call x1, Pallas kernels, shards(): pl.pallas_call(kernel, out_shape=jax.ShapeDtypeStruct((OWN, *tile), jnp.f...  50.9 us
    unnamed x2, local copies, waits for them, and re-layouts  3.2 us

profile of v1, /device:TPU:1, one launch (start us, length us, event | category | flops | bytes accessed | tf_op | source)
XLA Modules:
  0.0 54.1 jit_solution(12756497946131421477)
XLA Ops:
  0.0 1.3 %copy.8.dest = s32[16,1]{1,0:T(8,128)} copy(s32[16,1]{0,1:T(1,128)} %param.12) | data formatting | bytes 128 | tf_op args[5]
  1.3 50.9 %shard_map.73 = f32[8,128,128]{2,1,0:T(8,128)} custom-call(s32[16,48]{1,0:T(8,128)} %amp_ix.1, s32[16,48]{1,0:T(8,128)} %left_ix.1, s32[16,48]{1,0:T(8,128)} %right_ix.1, s32[16,1]{1,0:T(8,128)} %copy.8.dest, s32[16]{0:T(128)} %slot.1, bf16[4,128,128]{2,1,0:T(8,128)(2,1)} %amp_hbm.1, bf16[128,128,128]{2,1,0:T(8,128)(2,1)} %int_hbm.1), custom_call_target="tpu_custom_call" | custom-call | tf_op jit(solution)/shard_map/pallas_call | solution.py:317
  52.2 1.9 %copy.10 = f32[8,128,128]{2,1,0:T(8,128)} copy(f32[8,128,128]{2,1,0:T(8,128)} %shard_map.73) | data formatting | bytes 1048576

commit v2 on v1

v2 whole, which is shorter than its diff:
```python
import jax
import jax.numpy as jnp
from jax import lax
from jax.experimental import pallas as pl
from jax.experimental.pallas import tpu as pltpu
from jax.sharding import PartitionSpec as P

MESH = pl.DeviceIdType.MESH
OWN = 8
AMP = 4
X, Y, ZLO = 4, 4, 4
COLS = X * ZLO
EARLY = COLS // 2
SELF = COLS - 1
CHUNKS = 4


def product(left, right):
    return jnp.dot(left, right, preferred_element_type=jnp.float32)


def flip(bit):
    return 1 - bit


def other_half(row, far):
    return lax.rem(row + far * Y, 2 * Y)


def next_y(row, step):
    return (row // Y) * Y + lax.rem(row + step, Y)


def destination(col, place):
    x, z = col // ZLO, col % ZLO
    half, swap, dx = flip(place // EARLY), flip((place % EARLY) // X), (place + 1) % X
    z = lax.rem(z + 2 * half, ZLO)
    z = z + swap * (1 - 2 * (z % 2))
    return lax.rem(x + dx, X) * ZLO + z


def kernel(amp_in, left_in, right_in, dest_in, slot_in, amp_hbm, int_hbm, result_ref,
           amp_ix, left_ix, right_ix, dest, slot, amps, ints, turned, part, stage_s, stage_i, got_s, got_i, got_f, tags, tags_in,
           order, first, count,
           local_sem, y_send, y_recv, z_send, z_recv, zy_send, zy_recv, f_send, f_recv,
           s_send, s_recv, i_send, i_recv, b_send, b_recv, t_send, t_recv, out, out_sem):
    layer, row, col = lax.axis_index("layer"), lax.axis_index("row"), lax.axis_index("col")
    slots, terms = amp_ix.shape
    tiles = int_hbm.shape[0]
    edge = int_hbm.shape[1]
    half = AMP // 2
    mine = half * layer
    mate = {"layer": flip(layer)}
    far = other_half(row, 1)

    barrier = pltpu.get_barrier_semaphore()
    peers = [mate, {"row": far}]
    peers += [{"row": next_y(row, s)} for s in range(1, Y)]
    for peer in peers:
        pl.semaphore_signal(barrier, inc=1, device_id=peer, device_id_type=MESH)
    for place in range(COLS):
        if place != SELF:
            pl.semaphore_signal(barrier, inc=1, device_id={"col": destination(col, place)}, device_id_type=MESH)

    own_amp = pltpu.make_async_copy(amp_hbm, amps.at[pl.ds(row * AMP, AMP)], local_sem.at[CHUNKS])
    own_amp.start()
    tables = []
    for n, (src, dst) in enumerate(
        ((dest_in, dest), (slot_in, slot), (amp_in, amp_ix), (left_in, left_ix), (right_in, right_ix))
    ):
        tables.append(pltpu.make_async_copy(src, dst, local_sem.at[CHUNKS + 1 + n]))
        tables[-1].start()
    loads = []
    step = tiles // CHUNKS
    for c in range(CHUNKS):
        loads.append(pltpu.make_async_copy(int_hbm.at[pl.ds(c * step, step)], ints.at[pl.ds(c * step, step)], local_sem.at[c]))
        loads[-1].start()

    def turn(c):
        loads[c].wait()

        def four(i, _):
            for j in range(4):
                turned[c * step + 4 * i + j] = ints[c * step + 4 * i + j].T
            return 0

        lax.fori_loop(0, step // 4, four, 0)

    turn(0)
    own_amp.wait()
    pl.semaphore_wait(barrier, len(peers) + COLS - 1)

    def block(r, n=half, at=0):
        return amps.at[pl.ds(r * AMP + mine + at, n)]

    def send(src, dst, out_sem, in_sem, peer):
        return pltpu.make_async_remote_copy(
            src_ref=src, dst_ref=dst, send_sem=out_sem, recv_sem=in_sem, device_id=peer, device_id_type=MESH
        )

    z_copies = [send(block(row, 1, t), block(row, 1, t), z_send.at[t], z_recv.at[t], {"row": far}) for t in range(half)]
    for c in z_copies:
        c.start()
    y_copies = [
        send(block(row), block(row), y_send.at[s - 1], y_recv.at[s - 1], {"row": next_y(row, s)}) for s in (1, 3, 2)
    ]
    for c in y_copies:
        c.start()
    x, z = col // ZLO, col % ZLO

    def place_of(k):
        to = dest[k]
        dx = lax.rem(to // ZLO - x + 2 * X - 1, X)
        zt = lax.rem(to, ZLO)
        same = jnp.where(zt // 2 == z // 2, 1, 0)
        even = jnp.where(zt % 2 == z % 2, 1, 0)
        return same * EARLY + even * X + dx

    for c in tables:
        c.wait()
    places = [place_of(k) for k in range(slots)]
    ranks = []
    for k in range(slots):
        rank = 0
        for j in range(slots):
            if j < k:
                rank = rank + jnp.where(places[j] <= places[k], 1, 0)
            elif j > k:
                rank = rank + jnp.where(places[j] < places[k], 1, 0)
        ranks.append(rank)
    for i in range(slots):
        at, below, same = 0, 0, 0
        for k in range(slots):
            at = at + jnp.where(ranks[k] == i, k, 0)
            below = below + jnp.where(places[k] < i, 1, 0)
            same = same + jnp.where(places[k] == i, 1, 0)
        order[i] = at
        first[i] = below
        count[i] = same

    turn(1)
    to_mate = []

    def forward(r, n, at, k):
        to_mate.append(send(block(r, n, at), block(r, n, at), f_send.at[k], f_recv.at[k], mate))
        to_mate[-1].start()

    def arrived(r, n, at, sem):
        send(block(r, n, at), block(r, n, at), f_send.at[0], sem, mate).wait_recv()

    came = []

    def take(r, n, at, sem):
        arrived(r, n, at, sem)
        forward(r, n, at, len(came))
        came.append((r, n, at, len(came)))

    zy_copies = []
    for t in range(half):
        arrived(far, 1, t, z_recv.at[t])
        for s in (2, 1, 3):
            zy_copies.append(send(block(far, 1, t), block(far, 1, t), zy_send.at[t, s - 1], zy_recv.at[t, s - 1],
                                  {"row": next_y(row, s)}))
            zy_copies[-1].start()
        forward(far, 1, t, len(came))
        came.append((far, 1, t, len(came)))
    for s in (1, 3, 2):
        take(next_y(row, Y - s), half, 0, y_recv.at[s - 1])
    for c in range(2, CHUNKS):
        turn(c)

    def pick(place, j):
        at = jnp.minimum(first[place] + j, slots - 1)
        return at, j < count[place]

    def tag(place, _):
        for j in range(2):
            at, there = pick(place, j)
            tags[place, j] = jnp.full((8, edge), jnp.where(there, slot[order[at]], OWN), jnp.int32)
        return 0

    lax.fori_loop(0, COLS, tag, 0)

    tag_copies = []
    for place in range(COLS):
        if place != SELF:
            tag_copies.append(send(tags.at[place], tags_in.at[place], t_send.at[place], t_recv.at[place],
                                   {"col": destination(col, place)}))
            tag_copies[-1].start()

    for t in range(half):
        for s in (1, 3, 2):
            take(next_y(far, Y - s), 1, t, zy_recv.at[t, s - 1])

    def of_mate(r, n, at):
        return amps.at[pl.ds(r * AMP + half * flip(layer) + at, n)]

    for r, n, at, k in came:
        send(of_mate(r, n, at), of_mate(r, n, at), f_send.at[0], f_recv.at[k], mate).wait_recv()
    for c in z_copies + y_copies + zy_copies + to_mate:
        c.wait_send()

    def s_copy(p):
        return send(stage_s.at[p], got_s.at[p], s_send.at[p], s_recv.at[p], mate)

    def i_copy(p):
        return send(stage_i.at[p], got_i.at[p], i_send.at[p], i_recv.at[p], {"col": destination(col, p)})

    def b_copy(p):
        return send(got_i.at[p], got_f.at[p], b_send.at[p], b_recv.at[p], mate)

    def chosen(p, j):
        at, there = pick(p, j)
        return part[at] * jnp.where(there, 1.0, 0.0)

    def add_sibling(i):
        part[i] += got_s[i].astype(jnp.float32)

    def stage_owner(p):
        stage_i[p] = chosen(p, layer).astype(jnp.bfloat16)

    def to_owner(p):
        stage_owner(p)
        i_copy(p).start()

    def result(i):
        k = order[i]
        middles, lefts = [], []
        for t in range(terms):
            middles.append(product(amps[amp_ix[k, t]], turned[right_ix[k, t]]).astype(jnp.bfloat16))
            lefts.append(ints[left_ix[k, t]])
        part[i] = product(jnp.concatenate(lefts, 1), jnp.concatenate(middles, 0))

    def two(i):
        for k in (2 * i, 2 * i + 1):
            result(k)
        for k in (2 * i, 2 * i + 1):
            stage_s[k] = part[k].astype(jnp.bfloat16)

    def start_two(i):
        for k in (2 * i, 2 * i + 1):
            s_copy(k).start()

    def opening(i, _):
        two(i)
        start_two(i)
        return 0

    def steady(i, _):
        for k in (2 * i - 4, 2 * i - 3):
            s_copy(k).wait_recv()
        for k in (2 * i - 4, 2 * i - 3):
            add_sibling(k)
        stage_owner(i - 2)
        two(i)
        start_two(i)
        i_copy(i - 2).start()
        return 0

    lax.fori_loop(0, 2, opening, 0)
    lax.fori_loop(2, slots // 2, steady, 0)
    for k in (slots - 4, slots - 3):
        s_copy(k).wait_recv()
        add_sibling(k)
    to_owner(EARLY - 2)
    for k in (slots - 2, slots - 1):
        s_copy(k).wait_recv()
        add_sibling(k)
    to_owner(EARLY - 1)

    def rest(p, _):
        to_owner(p)
        return 0

    lax.fori_loop(EARLY, SELF, rest, 0)
    got_i[SELF] = chosen(SELF, layer).astype(jnp.bfloat16)
    b_copy(SELF).start()
    for place in range(COLS):
        if place != SELF:
            send(tags.at[place], tags_in.at[place], t_send.at[place], t_recv.at[place], mate).wait_recv()
    tags_in[SELF] = tags[SELF]

    def add(p, ref, j):
        label = tags_in[p, j]
        tile = ref[p].astype(jnp.float32).reshape(edge // 8, 8, edge)
        for s in range(OWN):
            there = jnp.where(label == s, 1.0, 0.0)
            out[s] += (tile * there[None]).reshape(edge, edge)

    def onward(p, _):
        i_copy(p).wait_recv()
        b_copy(p).start()
        return 0

    def onward_add(p, _):
        onward(p, 0)
        add(p, got_i, layer)
        return 0

    def add_own(p, _):
        add(p, got_i, layer)
        return 0

    def add_mate(p, _):
        b_copy(p).wait_recv()
        add(p, got_f, flip(layer))
        return 0

    lax.fori_loop(0, EARLY - 1, onward, 0)
    out[...] = jnp.zeros_like(out)
    add_own(SELF, 0)
    lax.fori_loop(0, EARLY - 1, add_own, 0)
    add_mate(SELF, 0)
    lax.fori_loop(0, EARLY - 1, add_mate, 0)
    lax.fori_loop(EARLY - 1, SELF, onward_add, 0)
    lax.fori_loop(EARLY - 1, SELF, add_mate, 0)

    final = pltpu.make_async_copy(out, result_ref, out_sem)
    final.start()

    def drain(p, _):
        s_copy(p).wait_send()
        b_copy(p).wait_send()
        return 0

    lax.fori_loop(0, COLS, drain, 0)
    for place in range(COLS):
        if place != SELF:
            i_copy(place).wait_send()
    for c in tag_copies:
        c.wait_send()
    final.wait()


def shards(amplitudes, integrals, amp_index, left_index, right_index, dest_col, owner_slot):
    edge = integrals.shape[1]
    half = AMP // 2
    rows = lax.axis_size("row")
    tile = (edge, edge)
    dma = pltpu.SemaphoreType.DMA
    in_hbm = pl.BlockSpec(memory_space=pl.ANY)
    forwards = 3 + half + 3 * half
    return pl.pallas_call(
        kernel,
        out_shape=jax.ShapeDtypeStruct((OWN, *tile), jnp.float32),
        in_specs=[in_hbm] * 7,
        out_specs=pl.BlockSpec(memory_space=pl.ANY),
        scratch_shapes=[
            pltpu.SMEM(amp_index.shape, jnp.int32),
            pltpu.SMEM(left_index.shape, jnp.int32),
            pltpu.SMEM(right_index.shape, jnp.int32),
            pltpu.SMEM((COLS,), jnp.int32),
            pltpu.SMEM((COLS,), jnp.int32),
            pltpu.VMEM((rows * AMP, *tile), jnp.bfloat16),
            pltpu.VMEM(integrals.shape, jnp.bfloat16),
            pltpu.VMEM(integrals.shape, jnp.bfloat16),
            pltpu.VMEM((COLS, *tile), jnp.float32),
            pltpu.VMEM((COLS, *tile), jnp.bfloat16),
            pltpu.VMEM((COLS, *tile), jnp.bfloat16),
            pltpu.VMEM((COLS, *tile), jnp.bfloat16),
            pltpu.VMEM((COLS, *tile), jnp.bfloat16),
            pltpu.VMEM((COLS, *tile), jnp.bfloat16),
            pltpu.VMEM((COLS, 2, 8, edge), jnp.int32),
            pltpu.VMEM((COLS, 2, 8, edge), jnp.int32),
            pltpu.SMEM((COLS,), jnp.int32),
            pltpu.SMEM((COLS,), jnp.int32),
            pltpu.SMEM((COLS,), jnp.int32),
            dma((CHUNKS + 6,)),
            dma((3,)), dma((3,)),
            dma((half,)), dma((half,)),
            dma((half, 3)), dma((half, 3)),
            dma((forwards,)), dma((forwards,)),
            dma((COLS,)), dma((COLS,)),
            dma((COLS,)), dma((COLS,)),
            dma((COLS,)), dma((COLS,)),
            dma((COLS,)), dma((COLS,)),
            pltpu.VMEM((OWN, *tile), jnp.float32), dma(()),
        ],
        compiler_params=pltpu.CompilerParams(collective_id=0, has_side_effects=True, vmem_limit_bytes=24 << 20),
    )(
        *(
            pltpu.with_memory_space_constraint(v, pltpu.HBM)
            for v in (amp_index, left_index, right_index, dest_col.reshape(-1), owner_slot, amplitudes, integrals)
        )
    )


def solution(mesh):
    placed = (
        P(("row", "col"), None, None),
        P(("layer", "row", "col"), None, None),
        P(("layer", "row", "col"), None),
        P(("layer", "row", "col"), None),
        P(("layer", "row", "col"), None),
        P(("row", "col"), None),
        P(("row", "col")),
    )
    return jax.shard_map(
        shards, mesh=mesh, in_specs=placed, out_specs=P(("row", "col"), None, None), check_vma=False
    )
```

time: 54.3 us -> 48.6 us (0.90)
  Pallas kernels: 50.9 us -> 47.7 us
  local copies, waits for them, and re-layouts: 3.2 us -> 0.8 us
    pallas_call x1, Pallas kernels: 50.9 us -> 47.7 us  [shards(): pl.pallas_call(kernel, out_shape=jax.ShapeDtypeStruct((OWN, *tile), jnp.f...]
    unnamed x2 -> x1, local copies, waits for them, and re-layouts: 3.2 us -> 0.8 us
where the time goes in v2:
time: 48.6 us; the launch traced here: 48.5 us
  Pallas kernels  47.7 us (98%)
  local copies, waits for them, and re-layouts  0.8 us (2%)
    pallas_call x1, Pallas kernels, shards(): pl.pallas_call(kernel, out_shape=jax.ShapeDtypeStruct((OWN, *tile), jnp.f...  47.7 us

profile of v2, /device:TPU:1, one launch (start us, length us, event | category | flops | bytes accessed | tf_op | source)
XLA Modules:
  0.0 48.5 jit_solution(17542736392019548864)
XLA Ops:
  0.0 47.7 %shard_map.73 = f32[8,128,128]{2,1,0:T(8,128)S(1)} custom-call(s32[16,48]{1,0:T(8,128)} %amp_in.1, s32[16,48]{1,0:T(8,128)} %left_in.1, s32[16,48]{1,0:T(8,128)} %right_in.1, s32[16]{0:T(128)} %bitcast.1, s32[16]{0:T(128)} %slot_in.1, bf16[4,128,128]{2,1,0:T(8,128)(2,1)} %amp_hbm.1, bf16[128,128,128]{2,1,0:T(8,128)(2,1)} %int_hbm.1), custom_call_target="tpu_custom_call" | custom-call | tf_op jit(solution)/shard_map/pallas_call | solution.py:343
  47.7 0.8 %copy.9 = f32[8,128,128]{2,1,0:T(8,128)} copy(f32[8,128,128]{2,1,0:T(8,128)S(1)} %shard_map.73) | data formatting | bytes 1048576

commit v3 on v2

--- a/solution.py
+++ b/solution.py
@@ -251,10 +251,9 @@
             s_copy(k).wait_recv()
         for k in (2 * i - 4, 2 * i - 3):
             add_sibling(k)
-        stage_owner(i - 2)
+        to_owner(i - 2)
         two(i)
         start_two(i)
-        i_copy(i - 2).start()
         return 0
 
     lax.fori_loop(0, 2, opening, 0)

time: 48.6 us -> 48 us (0.988)
  Pallas kernels: 47.7 us -> 47.1 us
    pallas_call x1, Pallas kernels: 47.7 us -> 47.1 us  [shards(): pl.pallas_call(kernel, out_shape=jax.ShapeDtypeStruct((OWN, *tile), jnp.f...]
where the time goes in v3:
time: 48 us; the launch traced here: 47.9 us
  Pallas kernels  47.1 us (98%)
  local copies, waits for them, and re-layouts  0.8 us (2%)
    pallas_call x1, Pallas kernels, shards(): pl.pallas_call(kernel, out_shape=jax.ShapeDtypeStruct((OWN, *tile), jnp.f...  47.1 us

profile of v3, /device:TPU:1, one launch (start us, length us, event | category | flops | bytes accessed | tf_op | source)
XLA Modules:
  0.0 47.9 jit_solution(4219834937889235983)
XLA Ops:
  0.0 47.1 %shard_map.73 = f32[8,128,128]{2,1,0:T(8,128)S(1)} custom-call(s32[16,48]{1,0:T(8,128)} %amp_in.1, s32[16,48]{1,0:T(8,128)} %left_in.1, s32[16,48]{1,0:T(8,128)} %right_in.1, s32[16]{0:T(128)} %bitcast.1, s32[16]{0:T(128)} %slot_in.1, bf16[4,128,128]{2,1,0:T(8,128)(2,1)} %amp_hbm.1, bf16[128,128,128]{2,1,0:T(8,128)(2,1)} %int_hbm.1), custom_call_target="tpu_custom_call" | custom-call | tf_op jit(solution)/shard_map/pallas_call | solution.py:342
  47.1 0.8 %copy.9 = f32[8,128,128]{2,1,0:T(8,128)} copy(f32[8,128,128]{2,1,0:T(8,128)S(1)} %shard_map.73) | data formatting | bytes 1048576

commit v4 on v3

--- a/solution.py
+++ b/solution.py
@@ -197,8 +197,6 @@
 
     for r, n, at, k in came:
         send(of_mate(r, n, at), of_mate(r, n, at), f_send.at[0], f_recv.at[k], mate).wait_recv()
-    for c in z_copies + y_copies + zy_copies + to_mate:
-        c.wait_send()
 
     def s_copy(p):
         return send(stage_s.at[p], got_s.at[p], s_send.at[p], s_recv.at[p], mate)
@@ -323,6 +321,8 @@
         return 0
 
     lax.fori_loop(0, COLS, drain, 0)
+    for c in z_copies + y_copies + zy_copies + to_mate:
+        c.wait_send()
     for place in range(COLS):
         if place != SELF:
             i_copy(place).wait_send()

time: 48 us -> 47.6 us (level)
  no operation moved by 1% of the time
where the time goes in v4:
time: 47.6 us; the launch traced here: 47.5 us
  Pallas kernels  46.7 us (98%)
  local copies, waits for them, and re-layouts  0.8 us (2%)
    pallas_call x1, Pallas kernels, shards(): pl.pallas_call(kernel, out_shape=jax.ShapeDtypeStruct((OWN, *tile), jnp.f...  46.7 us

profile of v4, /device:TPU:1, one launch (start us, length us, event | category | flops | bytes accessed | tf_op | source)
XLA Modules:
  0.0 47.5 jit_solution(4842360483132996743)
XLA Ops:
  0.0 46.7 %shard_map.73 = f32[8,128,128]{2,1,0:T(8,128)S(1)} custom-call(s32[16,48]{1,0:T(8,128)} %amp_in.1, s32[16,48]{1,0:T(8,128)} %left_in.1, s32[16,48]{1,0:T(8,128)} %right_in.1, s32[16]{0:T(128)} %bitcast.1, s32[16]{0:T(128)} %slot_in.1, bf16[4,128,128]{2,1,0:T(8,128)(2,1)} %amp_hbm.1, bf16[128,128,128]{2,1,0:T(8,128)(2,1)} %int_hbm.1), custom_call_target="tpu_custom_call" | custom-call | tf_op jit(solution)/shard_map/pallas_call | solution.py:342
  46.8 0.8 %copy.9 = f32[8,128,128]{2,1,0:T(8,128)} copy(f32[8,128,128]{2,1,0:T(8,128)S(1)} %shard_map.73) | data formatting | bytes 1048576

commit v5 on v4

--- a/solution.py
+++ b/solution.py
@@ -54,7 +54,7 @@
     far = other_half(row, 1)
 
     barrier = pltpu.get_barrier_semaphore()
-    peers = [mate, {"row": far}]
+    peers = [{"row": far}, mate]
     peers += [{"row": next_y(row, s)} for s in range(1, Y)]
     for peer in peers:
         pl.semaphore_signal(barrier, inc=1, device_id=peer, device_id_type=MESH)
@@ -86,7 +86,6 @@
 
         lax.fori_loop(0, step // 4, four, 0)
 
-    turn(0)
     own_amp.wait()
     pl.semaphore_wait(barrier, len(peers) + COLS - 1)
 
@@ -138,7 +137,8 @@
         first[i] = below
         count[i] = same
 
-    turn(1)
+    for c in range(2):
+        turn(c)
     to_mate = []
 
     def forward(r, n, at, k):
@@ -260,6 +260,12 @@
         s_copy(k).wait_recv()
         add_sibling(k)
     to_owner(EARLY - 2)
+    def onward(p, _):
+        i_copy(p).wait_recv()
+        b_copy(p).start()
+        return 0
+
+    lax.fori_loop(0, EARLY - 3, onward, 0)
     for k in (slots - 2, slots - 1):
         s_copy(k).wait_recv()
         add_sibling(k)
@@ -284,11 +290,6 @@
             there = jnp.where(label == s, 1.0, 0.0)
             out[s] += (tile * there[None]).reshape(edge, edge)
 
-    def onward(p, _):
-        i_copy(p).wait_recv()
-        b_copy(p).start()
-        return 0
-
     def onward_add(p, _):
         onward(p, 0)
         add(p, got_i, layer)
@@ -303,7 +304,7 @@
         add(p, got_f, flip(layer))
         return 0
 
-    lax.fori_loop(0, EARLY - 1, onward, 0)
+    lax.fori_loop(EARLY - 3, EARLY - 1, onward, 0)
     out[...] = jnp.zeros_like(out)
     add_own(SELF, 0)
     lax.fori_loop(0, EARLY - 1, add_own, 0)

time: 47.6 us -> 47.6 us (level)
  no operation moved by 1% of the time
where the time goes in v5:
time: 47.6 us; the launch traced here: 47.5 us
  Pallas kernels  46.7 us (98%)
  local copies, waits for them, and re-layouts  0.8 us (2%)
    pallas_call x1, Pallas kernels, shards(): pl.pallas_call(kernel, out_shape=jax.ShapeDtypeStruct((OWN, *tile), jnp.f...  46.7 us

profile of v5, /device:TPU:1, one launch (start us, length us, event | category | flops | bytes accessed | tf_op | source)
XLA Modules:
  0.0 47.5 jit_solution(13889394895133114391)
XLA Ops:
  0.0 46.7 %shard_map.73 = f32[8,128,128]{2,1,0:T(8,128)S(1)} custom-call(s32[16,48]{1,0:T(8,128)} %amp_in.1, s32[16,48]{1,0:T(8,128)} %left_in.1, s32[16,48]{1,0:T(8,128)} %right_in.1, s32[16]{0:T(128)} %bitcast.1, s32[16]{0:T(128)} %slot_in.1, bf16[4,128,128]{2,1,0:T(8,128)(2,1)} %amp_hbm.1, bf16[128,128,128]{2,1,0:T(8,128)(2,1)} %int_hbm.1), custom_call_target="tpu_custom_call" | custom-call | tf_op jit(solution)/shard_map/pallas_call | solution.py:343
  46.8 0.8 %copy.9 = f32[8,128,128]{2,1,0:T(8,128)} copy(f32[8,128,128]{2,1,0:T(8,128)S(1)} %shard_map.73) | data formatting | bytes 1048576
